TPU v7x, 32 devices: a whole 2x2x4 slice. The times are simulated.
32 devices in a mesh: in: 8 (over z, y), out: 4 (over x, core).
Axes of the slice: x: 2, y: 2, z: 4, core: 2. Of those that a mesh axis runs over, the one named last changes fastest.
Arguments:
- inputs: bfloat16 [64, 12288], P('out', 'in'), may hold values from -6 to 6
- weight: float32 [12288, 36864], P('in', 'out'), may hold values from -6 to 6
- out_grad: bfloat16 [64, 36864], P('in', 'out'), may hold values from -6 to 6
- step_size: float32 [], replicated, may hold values from 1 to 8
Outputs:
- projected: bfloat16 [64, 36864], P('in', 'out')
- input_grad: bfloat16 [64, 12288], P('out', 'in')
- new_weight: float32 [12288, 36864], P('in', 'out')
All inputs are finite; a program needn't handle non-finite values.
Results may differ from a plain program's by a relative error of at most 0.023.
Values may be sent and summed in bfloat16 or wider, within the bound.
A program may use at most 192 MiB of HBM per device.

v0:
```python
import jax
import jax.numpy as jnp
from jax import lax
from jax.sharding import PartitionSpec as P

D = 12288


def on_device(inputs, weight, out_grad, step_size):
    scale = float(D) ** (-0.5)
    low_weight = weight.astype(jnp.bfloat16)
    gathered = lax.all_gather(inputs, "out", axis=0, tiled=True)
    block = gathered
    summed = lax.psum_scatter(
        (jnp.dot(block, low_weight, preferred_element_type=jnp.float32) * scale)
        .astype(jnp.bfloat16)
        .astype(jnp.bfloat16),
        "in",
        scatter_dimension=0,
        tiled=True,
    )
    grad_all = lax.all_gather(out_grad, "in", axis=0, tiled=True)
    block = grad_all
    back = lax.dot_general(
        block, low_weight, (((1,), (1,)), ((), ())), preferred_element_type=jnp.float32
    )
    input_grad = lax.psum_scatter(
        (back * scale).astype(jnp.bfloat16).astype(jnp.bfloat16),
        "out",
        scatter_dimension=0,
        tiled=True,
    )
    weight_grad = (
        lax.dot_general(
            gathered, grad_all, (((0,), (0,)), ((), ())), preferred_element_type=jnp.float32
        )
        * scale
    )
    new_weight = weight - step_size * weight_grad
    return (summed, input_grad, new_weight)


def solution(mesh):
    placed = (P("out", "in"), P("in", "out"), P("in", "out"), P())
    return jax.shard_map(
        on_device,
        mesh=mesh,
        in_specs=placed,
        out_specs=(P("in", "out"), P("out", "in"), P("in", "out")),
        check_vma=False,
    )
```

profile of v0, /device:TPU:0, one launch (start us, length us, event | category | flops | bytes accessed | tf_op | source)
XLA Modules:
  0.0 149.9 jit_solution(2794381664677190572)
XLA Ops:
  7.2 0.0 all-gather.2.cloned.1.call-start
  7.2 0.7 all-gather.2.cloned.1.call-update
  7.9 0.0 reduce-scatter.3.cloned.1.call-start
  7.9 7.1 %all_gather.6 = bf16[64,1536]{1,0:T(8,128)(2,1)S(1)} all-gather(bf16[16,1536]{1,0:T(8,128)(2,1)} %param.4), channel_id=1, replica_groups=mesh['in'=8,'out'=4] {'out'}, dimensions={0}, use_global_device_ids=true | all-gather | bytes 245760 | tf_op jit(solution)/shard_map/all_gather | solution.py:12
  15.0 20.5 %fusion.7 = bf16[64,9216]{1,0:T(8,128)(2,1)} fusion(bf16[64,1536]{1,0:T(8,128)(2,1)S(1)} %all_gather.6, f32[1536,9216]{1,0:T(8,128)} %param.5), kind=kOutput, calls=%fused_computation.6 | convolution fusion | flops 1827274752 | bytes 57999360 | tf_op jit(solution)/shard_map/dot_general | solution.py:15
  35.5 0.0 reduce-scatter.3.cloned.1.call-update
  35.6 0.0 reduce-scatter.5.cloned.1.call-start
  36.3 17.8 %all-gather.2.cloned.1.call-done = bf16[64,9216]{1,0:T(8,128)(2,1)} async-done(((bf16[8,9216]{1,0:T(8,128)(2,1)}), bf16[64,9216]{1,0:T(8,128)(2,1)}) %all-gather.2.cloned.1.call-update) | async-done | bytes 1179664 | tf_op jit(solution)/shard_map/all_gather | solution.py:22
  54.1 0.0 copy-start
  54.1 24.9 %fusion.13 = bf16[64,1536]{1,0:T(8,128)(2,1)} fusion(bf16[64,9216]{1,0:T(8,128)(2,1)} %all-gather.2.cloned.1.call-done, f32[1536,9216]{1,0:T(8,128)} %param.5), kind=kOutput, calls=%fused_computation.8 | convolution fusion | flops 1826291712 | bytes 57999360 | tf_op jit(solution)/shard_map/dot_general | solution.py:24
  79.0 0.0 reduce-scatter.5.cloned.1.call-update
  79.0 0.0 copy-done
  79.0 37.0 %multiply_subtract_fusion = f32[1536,9216]{1,0:T(8,128)} fusion(f32[1536,9216]{1,0:T(8,128)} %param.5, bf16[64,1536]{1,0:T(8,128)(2,1)S(1)} %all_gather.6, bf16[64,9216]{1,0:T(8,128)(2,1)S(1)} %copy-done, f32[]{:T(128)S(6)} %mul.26), kind=kOutput, calls=%fused_computation | convolution fusion | flops 1840250880 | bytes 114622464 | tf_op jit(solution)/shard_map/dot_general | solution.py:34
  116.0 5.6 %reduce-scatter.3.cloned.1.call-done = bf16[8,9216]{1,0:T(8,128)(2,1)} async-done(((bf16[64,9216]{1,0:T(8,128)(2,1)}), bf16[8,9216]{1,0:T(8,128)(2,1)}) %reduce-scatter.3.cloned.1.call-update) | async-done | bytes 147472 | tf_op jit(solution)/shard_map/reduce_scatter | solution.py:14
  121.6 21.7 %reduce-scatter.5.cloned.1.call-done = bf16[16,1536]{1,0:T(8,128)(2,1)} async-done(((bf16[64,1536]{1,0:T(8,128)(2,1)}), bf16[16,1536]{1,0:T(8,128)(2,1)}) %reduce-scatter.5.cloned.1.call-update) | async-done | bytes 49168 | tf_op jit(solution)/shard_map/reduce_scatter | solution.py:27
Async XLA Ops:
  7.2 46.9 %all-gather.2.cloned.1.call-start = ((), (), s32[]{:S(2)}) async-start(), calls=%async_computation.3 | async-start | bytes 1327104 | tf_op jit(solution)/shard_map/all_gather | solution.py:22
  7.9 113.7 %reduce-scatter.3.cloned.1.call-start = ((), (), s32[]{:S(2)}) async-start(), calls=%async_computation.2 | async-start | bytes 1327104 | tf_op jit(solution)/shard_map/reduce_scatter | solution.py:14
  35.6 107.8 %reduce-scatter.5.cloned.1.call-start = ((), (), s32[]{:S(2)}) async-start(), calls=%async_computation.4 | async-start | bytes 245760 | tf_op jit(solution)/shard_map/reduce_scatter | solution.py:27
  54.1 24.9 %copy-start = (bf16[64,9216]{1,0:T(8,128)(2,1)S(1)}, bf16[64,9216]{1,0:T(8,128)(2,1)}, u32[]{:S(2)}) copy-start(bf16[64,9216]{1,0:T(8,128)(2,1)} %all-gather.2.cloned.1.call-done) | copy-start | bytes 3538948
Sparse Core Ops, SparseCore 0:
  10.2 43.8 all-gather.1
  58.0 63.5 reduce-scatter.2
  124.6 18.6 reduce-scatter.4
where the time goes:
time: 150 us
  matrix products  82.4 us (55%)
  waiting for transfers between devices  45.9 us (31%)
  between operations  14.4 us (10%)
  blocking collectives  7.08 us (5%)
    dot_general x1, matrix products, on_device(): lax.dot_general(gathered, grad_all, (((0,), (0,)), ((), ())), preferred_e...  37 us
    dot_general x1, matrix products, on_device(): lax.dot_general(block, low_weight, (((1,), (1,)), ((), ())), preferred_el...  24.9 us
    reduce_scatter x1, waiting for transfers between devices, on_device(): lax.psum_scatter((back * scale).astype(jnp.bfloat16).astype(jnp.bfloat16)...  21.7 us
    dot_general x1, matrix products, on_device(): jnp.dot(block, low_weight, preferred_element_type=jnp.float32) * scale  20.5 us
    all_gather x1, waiting for transfers between devices, on_device(): grad_all = lax.all_gather(out_grad, 'in', axis=0, tiled=True)  17.8 us
    all_gather x1, blocking collectives, on_device(): gathered = lax.all_gather(inputs, 'out', axis=0, tiled=True)  7.08 us
    reduce_scatter x1, waiting for transfers between devices, on_device(): lax.psum_scatter((jnp.dot(block, low_weight, preferred_element_type=jnp.f...  5.61 us
  transfers between devices with their start and end apart: 3, of which 3 were waited for; matrix products, arithmetic and copies ran while one was open for 55% of the time, Pallas kernels for 0%

commit v1 on v0

--- a/solution.py
+++ b/solution.py
@@ -19,7 +19,12 @@
         scatter_dimension=0,
         tiled=True,
     )
-    grad_all = lax.all_gather(out_grad, "in", axis=0, tiled=True)
+    ring = [out_grad]
+    for hop in range(7):
+        ring.append(lax.ppermute(ring[-1], "in", [(dev, (dev + 1) % 8) for dev in range(8)]))
+    grad_all = jnp.roll(
+        jnp.concatenate(ring[::-1], axis=0), (lax.axis_index("in") + 1) * ring[0].shape[0], axis=0
+    )
     block = grad_all
     back = lax.dot_general(
         block, low_weight, (((1,), (1,)), ((), ())), preferred_element_type=jnp.float32

time: 150 us -> 266 us (1.77)
  local copies, waits for them, and re-layouts: 0.01 us -> 113 us
  matrix products: 82.4 us -> 78.1 us
  waiting for transfers between devices: 45.9 us -> 49.6 us
  starting transfers between devices: 0.12 us -> 3.14 us
    unnamed x2 -> x23, local copies, waits for them, and re-layouts: 0.01 us -> 113 us
    ppermute x0 -> x7, waiting for transfers between devices: none -> 49.5 us  [on_device(): lax.ppermute(ring[-1], 'in', [(dev, (dev + 1) % 8) for dev in range(8)])]
    reduce_scatter x1, waiting for transfers between devices: 21.7 us -> 0.01 us  [on_device(): lax.psum_scatter((back * scale).astype(jnp.bfloat16).astype(jnp.bfloat16)...]
    all_gather x1 -> x0, waiting for transfers between devices: 17.8 us -> none  [on_device(): grad_all = lax.all_gather(out_grad, 'in', axis=0, tiled=True)]
    reduce_scatter x1, waiting for transfers between devices: 5.61 us -> 0.01 us  [on_device(): lax.psum_scatter((jnp.dot(block, low_weight, preferred_element_type=jnp.f...]
    dot_general x1, matrix products: 24.9 us -> 21 us  [on_device(): lax.dot_general(block, low_weight, (((1,), (1,)), ((), ())), preferred_el...]
    ppermute x0 -> x7, starting transfers between devices: none -> 3.06 us  [on_device(): lax.ppermute(ring[-1], 'in', [(dev, (dev + 1) % 8) for dev in range(8)])]
  transfers between devices with their start and end apart: 3 -> 9, of which waited for: 3 -> 7; matrix products, arithmetic and copies ran while one was open for 55% -> 63% of each run, Pallas kernels for 0% -> 0%
where the time goes in v1:
time: 266 us; the launch traced here: 264 us
  local copies, waits for them, and re-layouts  113 us (42%)
  matrix products  78.1 us (29%)
  waiting for transfers between devices  49.6 us (19%)
  between operations  14.8 us (6%)
  blocking collectives  5.92 us (2%)
  starting transfers between devices  3.14 us (1%)
    unnamed x23, local copies, waits for them, and re-layouts  113 us
    ppermute x7, waiting for transfers between devices, on_device(): lax.ppermute(ring[-1], 'in', [(dev, (dev + 1) % 8) for dev in range(8)])  49.5 us
    dot_general x1, matrix products, on_device(): lax.dot_general(gathered, grad_all, (((0,), (0,)), ((), ())), preferred_e...  36.5 us
    dot_general x1, matrix products, on_device(): lax.dot_general(block, low_weight, (((1,), (1,)), ((), ())), preferred_el...  21 us
    dot_general x1, matrix products, on_device(): jnp.dot(block, low_weight, preferred_element_type=jnp.float32) * scale  20.5 us
    all_gather x1, blocking collectives, on_device(): gathered = lax.all_gather(inputs, 'out', axis=0, tiled=True)  5.92 us
  transfers between devices with their start and end apart: 9, of which 7 were waited for; matrix products, arithmetic and copies ran while one was open for 63% of the time, Pallas kernels for 0%

profile of v1, /device:TPU:0, one launch (start us, length us, event | category | flops | bytes accessed | tf_op | source)
XLA Modules:
  0.0 264.4 jit_solution(128494367365207732)
XLA Ops:
  7.2 0.0 copy-start
  7.2 0.0 reduce-scatter.5.cloned.1.call-start
  7.2 3.0 %collective-permute-start = (bf16[8,9216]{1,0:T(8,128)(2,1)}, bf16[8,9216]{1,0:T(8,128)(2,1)S(1)}, u32[]{:S(2)}, u32[]{:S(2)}) collective-permute-start(bf16[8,9216]{1,0:T(8,128)(2,1)} %param.6), channel_id=1, source_target_pairs={{0,4},{4,8},{8,12},{12,16},{16,20},{20,24},{24,28},{28,0},{1,5},{5... | collective-permute-start | bytes 442376 | tf_op jit(solution)/shard_map/ppermute | solution.py:24
  10.3 7.1 %collective-permute-done = bf16[8,9216]{1,0:T(8,128)(2,1)S(1)} collective-permute-done((bf16[8,9216]{1,0:T(8,128)(2,1)}, bf16[8,9216]{1,0:T(8,128)(2,1)S(1)}, u32[]{:S(2)}, u32[]{:S(2)}) %collective-permute-start) | collective-permute-done | bytes 147488 | tf_op jit(solution)/shard_map/ppermute | solution.py:24
  17.4 0.0 collective-permute-start.1
  17.4 7.8 %collective-permute-done.1 = bf16[8,9216]{1,0:T(8,128)(2,1)S(1)} collective-permute-done((bf16[8,9216]{1,0:T(8,128)(2,1)S(1)}, bf16[8,9216]{1,0:T(8,128)(2,1)S(1)}, u32[]{:S(2)}, u32[]{:S(2)}) %collective-permute-start.1) | collective-permute-done | bytes 147488 | tf_op jit(solution)/shard_map/ppermute | solution.py:24
  25.2 0.0 collective-permute-start.2
  25.2 7.8 %collective-permute-done.2 = bf16[8,9216]{1,0:T(8,128)(2,1)S(1)} collective-permute-done((bf16[8,9216]{1,0:T(8,128)(2,1)S(1)}, bf16[8,9216]{1,0:T(8,128)(2,1)S(1)}, u32[]{:S(2)}, u32[]{:S(2)}) %collective-permute-start.2) | collective-permute-done | bytes 147488 | tf_op jit(solution)/shard_map/ppermute | solution.py:24
  33.0 0.0 collective-permute-start.3
  33.0 7.8 %collective-permute-done.3 = bf16[8,9216]{1,0:T(8,128)(2,1)S(1)} collective-permute-done((bf16[8,9216]{1,0:T(8,128)(2,1)S(1)}, bf16[8,9216]{1,0:T(8,128)(2,1)S(1)}, u32[]{:S(2)}, u32[]{:S(2)}) %collective-permute-start.3) | collective-permute-done | bytes 147488 | tf_op jit(solution)/shard_map/ppermute | solution.py:24
  40.9 0.0 collective-permute-start.4
  40.9 7.9 %collective-permute-done.4 = bf16[8,9216]{1,0:T(8,128)(2,1)S(1)} collective-permute-done((bf16[8,9216]{1,0:T(8,128)(2,1)S(1)}, bf16[8,9216]{1,0:T(8,128)(2,1)S(1)}, u32[]{:S(2)}, u32[]{:S(2)}) %collective-permute-start.4) | collective-permute-done | bytes 147488 | tf_op jit(solution)/shard_map/ppermute | solution.py:24
  48.8 0.0 collective-permute-start.5
  48.8 9.0 %collective-permute-done.5 = bf16[8,9216]{1,0:T(8,128)(2,1)S(1)} collective-permute-done((bf16[8,9216]{1,0:T(8,128)(2,1)S(1)}, bf16[8,9216]{1,0:T(8,128)(2,1)S(1)}, u32[]{:S(2)}, u32[]{:S(2)}) %collective-permute-start.5) | collective-permute-done | bytes 147488 | tf_op jit(solution)/shard_map/ppermute | solution.py:24
  57.8 0.0 copy-start.1
  57.8 0.0 collective-permute-start.6
  57.8 5.9 %all_gather.3 = bf16[64,1536]{1,0:T(8,128)(2,1)S(1)} all-gather(bf16[16,1536]{1,0:T(8,128)(2,1)} %param.4), channel_id=1, replica_groups=mesh['in'=8,'out'=4] {'out'}, dimensions={0}, use_global_device_ids=true | all-gather | bytes 245760 | tf_op jit(solution)/shard_map/all_gather | solution.py:12
  63.7 0.0 copy-done.1
  63.7 2.0 collective-permute-done.6
  65.7 0.0 copy-start.2
  65.8 1.0 constant_dynamic-update-slice_fusion.15
  66.7 0.9 constant_dynamic-update-slice_fusion.14
  67.7 0.0 copy-done
  67.8 0.9 constant_dynamic-update-slice_fusion.7
  68.7 0.0 copy-done.2
  68.8 21.0 %fusion.13 = bf16[64,1536]{1,0:T(8,128)(2,1)} fusion(f32[1536,9216]{1,0:T(8,128)} %param.5, bf16[128,9216]{1,0:T(8,128)(2,1)S(1)} %constant_dynamic-update-slice_fusion, s32[]{:T(128)S(6)} %select_n.14), kind=kOutput, calls=%fused_computation.8 | convolution fusion | flops 1826291712 | bytes 57999364 | tf_op jit(solution)/shard_map/dot_general | solution.py:29
  89.9 0.0 reduce-scatter.5.cloned.1.call-update
  89.9 0.0 reduce-scatter.3.cloned.1.call-start
  90.0 20.5 %fusion.7 = bf16[64,9216]{1,0:T(8,128)(2,1)} fusion(bf16[64,1536]{1,0:T(8,128)(2,1)S(1)} %all_gather.3, f32[1536,9216]{1,0:T(8,128)} %param.5), kind=kOutput, calls=%fused_computation.6 | convolution fusion | flops 1827274752 | bytes 57999360 | tf_op jit(solution)/shard_map/dot_general | solution.py:15
  110.5 0.0 reduce-scatter.3.cloned.1.call-update
  110.5 55.0 %copy.7 = f32[1536,9216]{0,1:T(8,128)} copy(f32[1536,9216]{1,0:T(8,128)} %param.5) | data formatting | bytes 113246208 | tf_op args[1]
  166.1 36.5 %bitcast_subtract_fusion = f32[1536,9216]{0,1:T(8,128)} fusion(f32[1536,9216]{0,1:T(8,128)} %copy.7, bf16[64,1536]{1,0:T(8,128)(2,1)S(1)} %all_gather.3, f32[]{:T(128)S(6)} %mul.33, bf16[128,9216]{1,0:T(8,128)(2,1)S(1)} %constant_dynamic-update-slice_fusion, s32[]{:T(128)S(6)} %select_n.14), kind=kOutput, calls=%fused_computation | convolution fusion | flops 1840250880 | bytes 114622472 | tf_op jit(solution)/shard_map/dot_general | solution.py:39
  202.7 54.9 %copy.8 = f32[1536,9216]{1,0:T(8,128)} copy(f32[1536,9216]{0,1:T(8,128)} %bitcast_subtract_fusion) | data formatting | bytes 113246208
  257.6 0.0 reduce-scatter.5.cloned.1.call-done
  257.6 0.0 reduce-scatter.3.cloned.1.call-done
  (13 shorter events, 0.2 us)
Async XLA Ops:
  7.2 60.6 %copy-start = (bf16[8,9216]{1,0:T(8,128)(2,1)S(1)}, bf16[8,9216]{1,0:T(8,128)(2,1)}, u32[]{:S(2)}) copy-start(bf16[8,9216]{1,0:T(8,128)(2,1)} %param.6) | copy-start | bytes 442372
  7.2 250.4 %reduce-scatter.5.cloned.1.call-start = ((), (), s32[]{:S(2)}) async-start(), calls=%async_computation.3 | async-start | bytes 245760 | tf_op jit(solution)/shard_map/reduce_scatter | solution.py:32
  7.2 10.1 %collective-permute-start = (bf16[8,9216]{1,0:T(8,128)(2,1)}, bf16[8,9216]{1,0:T(8,128)(2,1)S(1)}, u32[]{:S(2)}, u32[]{:S(2)}) collective-permute-start(bf16[8,9216]{1,0:T(8,128)(2,1)} %param.6), channel_id=1, source_target_pairs={{0,4},{4,8},{8,12},{12,16},{16,20},{20,24},{24,28},{28,0},{1,5},{5... | collective-permute-start | bytes 442376 | tf_op jit(solution)/shard_map/ppermute | solution.py:24
  17.4 7.8 %collective-permute-start.1 = (bf16[8,9216]{1,0:T(8,128)(2,1)S(1)}, bf16[8,9216]{1,0:T(8,128)(2,1)S(1)}, u32[]{:S(2)}, u32[]{:S(2)}) collective-permute-start(bf16[8,9216]{1,0:T(8,128)(2,1)S(1)} %collective-permute-done), channel_id=1, source_target_pairs={{0,4},{4,8},{8,12},{12,16},{16,20},{20,24},{24,28},{28,0},{1,5},{5... | collective-permute-start | bytes 442376 | tf_op jit(solution)/shard_map/ppermute | solution.py:24
  25.2 7.8 %collective-permute-start.2 = (bf16[8,9216]{1,0:T(8,128)(2,1)S(1)}, bf16[8,9216]{1,0:T(8,128)(2,1)S(1)}, u32[]{:S(2)}, u32[]{:S(2)}) collective-permute-start(bf16[8,9216]{1,0:T(8,128)(2,1)S(1)} %collective-permute-done.1), channel_id=1, source_target_pairs={{0,4},{4,8},{8,12},{12,16},{16,20},{20,24},{24,28},{28,0},{1,5},{5... | collective-permute-start | bytes 442376 | tf_op jit(solution)/shard_map/ppermute | solution.py:24
  33.0 7.8 %collective-permute-start.3 = (bf16[8,9216]{1,0:T(8,128)(2,1)S(1)}, bf16[8,9216]{1,0:T(8,128)(2,1)S(1)}, u32[]{:S(2)}, u32[]{:S(2)}) collective-permute-start(bf16[8,9216]{1,0:T(8,128)(2,1)S(1)} %collective-permute-done.2), channel_id=1, source_target_pairs={{0,4},{4,8},{8,12},{12,16},{16,20},{20,24},{24,28},{28,0},{1,5},{5... | collective-permute-start | bytes 442376 | tf_op jit(solution)/shard_map/ppermute | solution.py:24
  40.9 7.9 %collective-permute-start.4 = (bf16[8,9216]{1,0:T(8,128)(2,1)S(1)}, bf16[8,9216]{1,0:T(8,128)(2,1)S(1)}, u32[]{:S(2)}, u32[]{:S(2)}) collective-permute-start(bf16[8,9216]{1,0:T(8,128)(2,1)S(1)} %collective-permute-done.3), channel_id=1, source_target_pairs={{0,4},{4,8},{8,12},{12,16},{16,20},{20,24},{24,28},{28,0},{1,5},{5... | collective-permute-start | bytes 442376 | tf_op jit(solution)/shard_map/ppermute | solution.py:24
  48.8 9.0 %collective-permute-start.5 = (bf16[8,9216]{1,0:T(8,128)(2,1)S(1)}, bf16[8,9216]{1,0:T(8,128)(2,1)S(1)}, u32[]{:S(2)}, u32[]{:S(2)}) collective-permute-start(bf16[8,9216]{1,0:T(8,128)(2,1)S(1)} %collective-permute-done.4), channel_id=1, source_target_pairs={{0,4},{4,8},{8,12},{12,16},{16,20},{20,24},{24,28},{28,0},{1,5},{5... | collective-permute-start | bytes 442376 | tf_op jit(solution)/shard_map/ppermute | solution.py:24
  57.8 5.9 %copy-start.1 = (bf16[8,9216]{1,0:T(8,128)(2,1)}, bf16[8,9216]{1,0:T(8,128)(2,1)S(1)}, u32[]{:S(2)}) copy-start(bf16[8,9216]{1,0:T(8,128)(2,1)S(1)} %collective-permute-done.5) | copy-start | bytes 442372
  57.8 7.9 %collective-permute-start.6 = (bf16[8,9216]{1,0:T(8,128)(2,1)S(1)}, bf16[8,9216]{1,0:T(8,128)(2,1)}, u32[]{:S(2)}, u32[]{:S(2)}) collective-permute-start(bf16[8,9216]{1,0:T(8,128)(2,1)S(1)} %collective-permute-done.5), channel_id=1, source_target_pairs={{0,4},{4,8},{8,12},{12,16},{16,20},{20,24},{24,28},{28,0},{1,5},{5... | collective-permute-start | bytes 442376 | tf_op jit(solution)/shard_map/ppermute | solution.py:24
  65.7 2.9 %copy-start.2 = (bf16[8,9216]{1,0:T(8,128)(2,1)S(1)}, bf16[8,9216]{1,0:T(8,128)(2,1)}, u32[]{:S(2)}) copy-start(bf16[8,9216]{1,0:T(8,128)(2,1)} %copy-done.1) | copy-start | bytes 442372
  89.9 167.7 %reduce-scatter.3.cloned.1.call-start = ((), (), s32[]{:S(2)}) async-start(), calls=%async_computation.2 | async-start | bytes 1327104 | tf_op jit(solution)/shard_map/reduce_scatter | solution.py:14
Sparse Core Ops, SparseCore 0:
  90.0 19.3 reduce-scatter.4
  113.4 64.7 reduce-scatter.2
